TPU v7x, 256 devices: a whole 4x4x8 slice. The times are simulated.
256 devices in a mesh: dp: 4 (over z_lo, core), seq: 64 (over y, x, z_hi).
Axes of the slice: x: 4, y: 4, z: 8 (z_hi: 4, z_lo: 2; z = z_hi * 2 + z_lo), core: 2. Of those that a mesh axis runs over, the one named last changes fastest.
Arguments:
- traces_in: bfloat16 [8, 512, 512, 128], P('dp', 'seq'), may hold values from -6 to 6
- w_value: bfloat16 [128, 128], replicated, may hold values from -0.5 to 0.5
- w_gate: bfloat16 [128, 128], replicated, may hold values from -0.5 to 0.5
- first_blocks: bfloat16 [512, 512, 512], P('seq', 'dp'), may hold values from -0.25 to 0.25
- second_blocks: bfloat16 [512, 512, 512], P('seq', 'dp'), may hold values from -0.25 to 0.25
- cotangent: bfloat16 [8, 512, 512, 128], P('dp', 'seq'), may hold values from -6 to 6
Outputs:
- mixed: bfloat16 [8, 512, 512, 128], P('dp', 'seq')
- grad_in: bfloat16 [8, 512, 512, 128], P('dp', 'seq')
- grad_first: bfloat16 [512, 512, 512], P('seq', 'dp')
- grad_second: bfloat16 [512, 512, 512], P('seq', 'dp')
All inputs are finite; a program needn't handle non-finite values.
Results may differ from a plain program's by a relative error of at most 0.015.
Values may be sent and summed in bfloat16 or wider, within the bound.
A program may use at most 128 MiB of HBM per device.

v0:
```python
import jax
import jax.numpy as jnp
from jax import lax
from jax.sharding import PartitionSpec as P


def on_device(traces_in, w_value, w_gate, first_blocks, second_blocks, cotangent):
    full_first, full_second = (
        lax.all_gather(first_blocks, "dp", axis=1, tiled=True),
        lax.all_gather(second_blocks, "dp", axis=1, tiled=True),
    )
    values = jnp.einsum(
        "tpqc,cd->tpqd", traces_in, w_value, preferred_element_type=jnp.float32
    ).astype(jnp.bfloat16)
    gates = jnp.einsum("tpqc,cd->tpqd", traces_in, w_gate, preferred_element_type=jnp.float32)
    sig = jax.nn.sigmoid(gates)
    act = gates * sig
    rowmix = jnp.einsum(
        "pij,tpjc->tpic", full_first, values, preferred_element_type=jnp.float32
    ).astype(jnp.bfloat16)
    gradf = cotangent.astype(jnp.float32)
    d_col = (gradf * act).astype(jnp.bfloat16)
    columns = lax.all_to_all(rowmix, "seq", split_axis=2, concat_axis=1, tiled=True)
    mixed_cols = jnp.einsum(
        "qij,tjqc->tiqc", full_second, columns, preferred_element_type=jnp.float32
    )
    colmix_cols = mixed_cols.astype(jnp.bfloat16)
    colmix = lax.all_to_all(colmix_cols, "seq", split_axis=1, concat_axis=2, tiled=True)
    cotan_cols = lax.all_to_all(d_col, "seq", split_axis=2, concat_axis=1, tiled=True)
    back = jnp.einsum("qij,tiqc->tjqc", full_second, cotan_cols, preferred_element_type=jnp.float32)
    d_row_cols = back.astype(jnp.bfloat16)
    d_row = lax.all_to_all(d_row_cols, "seq", split_axis=1, concat_axis=2, tiled=True)
    colf = colmix.astype(jnp.float32)
    mixed = (colf * act).astype(jnp.bfloat16)
    d_gate = (gradf * colf * sig * (1.0 + gates * (1.0 - sig))).astype(jnp.bfloat16)
    d_val = jnp.einsum(
        "pij,tpic->tpjc", full_first, d_row, preferred_element_type=jnp.float32
    ).astype(jnp.bfloat16)
    grad_in = jnp.einsum("tpqd,cd->tpqc", d_val, w_value, preferred_element_type=jnp.float32)
    grad_in = (
        grad_in + jnp.einsum("tpqd,cd->tpqc", d_gate, w_gate, preferred_element_type=jnp.float32)
    ).astype(jnp.bfloat16)
    trace_count = traces_in.shape[0] * lax.axis_size("dp")
    second_part = jnp.einsum(
        "tiqc,tjqc->qij", cotan_cols, columns, preferred_element_type=jnp.float32
    )
    second_sum = lax.psum_scatter(
        second_part.astype(jnp.bfloat16), "dp", scatter_dimension=1, tiled=True
    ).astype(jnp.float32)
    first_part = jnp.einsum("tpic,tpjc->pij", d_row, values, preferred_element_type=jnp.float32)
    first_sum = lax.psum_scatter(
        first_part.astype(jnp.bfloat16), "dp", scatter_dimension=1, tiled=True
    ).astype(jnp.float32)
    grad_first = (first_sum / trace_count).astype(jnp.bfloat16)
    grad_second = (second_sum / trace_count).astype(jnp.bfloat16)
    return (mixed, grad_in, grad_first, grad_second)


def solution(mesh):
    return jax.shard_map(
        on_device,
        mesh=mesh,
        in_specs=(
            P("dp", "seq", None, None),
            P(),
            P(),
            P("seq", "dp", None),
            P("seq", "dp", None),
            P("dp", "seq", None, None),
        ),
        out_specs=(
            P("dp", "seq", None, None),
            P("dp", "seq", None, None),
            P("seq", "dp", None),
            P("seq", "dp", None),
        ),
        check_vma=False,
    )
```

profile of v0, /device:TPU:1, one launch (start us, length us, event | category | flops | bytes accessed | tf_op | source)
XLA Modules:
  0.0 446.5 jit_solution(18387896903272516224)
XLA Ops:
  7.2 0.0 copy-start
  7.2 0.0 copy-start.7
  7.2 0.0 all-gather.3.cloned.1.call-start
  7.2 0.7 all-gather.3.cloned.1.call-update
  7.9 0.0 all-gather.5.cloned.1.call-start
  8.0 0.7 all-gather.5.cloned.1.call-update
  8.7 0.0 reduce-scatter.5.cloned.1.call-start
  8.7 0.0 copy-done
  8.8 0.0 copy-done.7
  8.8 2.0 convolution_convert_fusion
  10.8 52.5 %all-gather.3.cloned.1.call-done = bf16[8,512,512]{2,1,0:T(8,128)(2,1)} async-done(((bf16[8,128,512]{2,1,0:T(8,128)(2,1)}), bf16[8,512,512]{2,1,0:T(8,128)(2,1)}) %all-gather.3.cloned.1.call-update) | async-done | bytes 4194320 | tf_op jit(solution)/shard_map/all_gather | solution.py:9
  63.3 5.5 %convert_bitcast_fusion.3 = bf16[2,8,512,128]{2,3,0,1:T(8,128)(2,1)} fusion(bf16[8,512,512]{2,1,0:T(8,128)(2,1)} %all-gather.3.cloned.1.call-done, bf16[2,8,512,128]{3,2,1,0:T(8,128)(2,1)} %convolution_convert_fusion), kind=kOutput, calls=%fused_computation.33 | convolution fusion | flops 1074790400 | bytes 8388608 | tf_op jit(solution)/shard_map/pij,tpjc->tpic/dot_general | solution.py:18
  68.7 6.2 %copy.50 = bf16[2,8,512,128]{3,0,1,2:T(2,128)(2,1)} copy(bf16[2,8,512,128]{2,3,0,1:T(8,128)(2,1)} %convert_bitcast_fusion.3) | data formatting | bytes 4194304 | tf_op jit(solution)/shard_map/convert_element_type | solution.py:20
  74.9 88.4 %all_to_all.63 = bf16[2,8,512,128]{3,0,1,2:T(2,128)(2,1)S(1)} all-to-all(bf16[2,8,512,128]{3,0,1,2:T(2,128)(2,1)} %copy.50), channel_id=1, replica_groups=mesh['dp'=4,'seq'=64] {'seq'}, dimensions={2} | all-to-all | bytes 4194304 | tf_op jit(solution)/shard_map/all_to_all | solution.py:23
  163.3 0.5 copy.103
  163.9 2.0 copy.52
  165.8 5.6 %convert_bitcast_fusion.2 = bf16[2,512,8,128]{1,3,0,2:T(8,128)(2,1)} fusion(bf16[8,512,512]{2,1,0:T(8,128)(2,1)} %all-gather.5.cloned.1.call-done, bf16[2,512,8,128]{3,2,1,0:T(8,128)(2,1)} %bitcast.92), kind=kOutput, calls=%fused_computation.32 | convolution fusion | flops 1074790400 | bytes 8388608 | tf_op jit(solution)/shard_map/qij,tjqc->tiqc/dot_general | solution.py:24
  171.4 6.2 %copy.54 = bf16[2,512,8,128]{3,0,2,1:T(2,128)(2,1)} copy(bf16[2,512,8,128]{1,3,0,2:T(8,128)(2,1)} %convert_bitcast_fusion.2) | data formatting | bytes 4194304 | tf_op jit(solution)/shard_map/convert_element_type | solution.py:27
  177.6 50.9 %all_to_all.64 = bf16[2,512,8,128]{3,0,2,1:T(2,128)(2,1)S(1)} all-to-all(bf16[2,512,8,128]{3,0,2,1:T(2,128)(2,1)} %copy.54), channel_id=1, replica_groups=mesh['dp'=4,'seq'=64] {'seq'}, dimensions={1} | all-to-all | bytes 4194304 | tf_op jit(solution)/shard_map/all_to_all | solution.py:28
  228.5 0.3 copy.55
  228.8 0.0 copy-start.6
  228.8 2.1 copy-done.8
  230.8 0.0 copy-done.9
  230.8 3.7 fusion
  234.5 0.0 copy-done.6
  234.5 1.4 copy.57
  235.9 38.6 %all_to_all.65 = bf16[2,8,512,128]{3,1,0,2:T(8,128)(2,1)S(1)} all-to-all(bf16[2,8,512,128]{3,1,0,2:T(8,128)(2,1)S(1)} %copy.57), channel_id=1, replica_groups=mesh['dp'=4,'seq'=64] {'seq'}, dimensions={2} | all-to-all | bytes 4194304 | tf_op jit(solution)/shard_map/all_to_all | solution.py:29
  274.5 0.8 copy.59
  275.3 0.0 copy-start.4
  275.3 1.3 copy-done.4
  276.7 0.0 copy-done.2
  276.7 3.3 bitcast_convert_fusion
  280.0 0.0 reduce-scatter.5.cloned.1.call-update
  280.0 0.0 reduce-scatter.3.cloned.1.call-start
  280.0 1.5 copy-done.5
  281.6 4.8 %convert_bitcast_fusion.1 = bf16[2,512,8,128]{1,3,0,2:T(8,128)(2,1)} fusion(bf16[8,512,512]{2,1,0:T(8,128)(2,1)} %all-gather.5.cloned.1.call-done, bf16[2,512,8,128]{3,2,1,0:T(8,128)(2,1)S(1)} %bitcast.97), kind=kOutput, calls=%fused_computation.31 | convolution fusion | flops 1074790400 | bytes 8388608 | tf_op jit(solution)/shard_map/qij,tiqc->tjqc/dot_general | solution.py:30
  286.4 4.9 %copy.61 = bf16[2,512,8,128]{3,0,2,1:T(2,128)(2,1)S(1)} copy(bf16[2,512,8,128]{1,3,0,2:T(8,128)(2,1)} %convert_bitcast_fusion.1) | data formatting | bytes 4194304 | tf_op jit(solution)/shard_map/convert_element_type | solution.py:31
  291.3 53.9 %all_to_all.66 = bf16[2,512,8,128]{3,0,2,1:T(2,128)(2,1)S(1)} all-to-all(bf16[2,512,8,128]{3,0,2,1:T(2,128)(2,1)S(1)} %copy.61), channel_id=1, replica_groups=mesh['dp'=4,'seq'=64] {'seq'}, dimensions={1} | all-to-all | bytes 4194304 | tf_op jit(solution)/shard_map/all_to_all | solution.py:32
  345.2 0.3 copy.62
  345.5 1.3 copy-done.3
  346.8 3.3 bitcast_convert_fusion.1
  350.1 0.0 reduce-scatter.3.cloned.1.call-update
  350.1 6.0 %fusion.14 = f32[2,8,512,128]{3,2,1,0:T(8,128)} fusion(bf16[8,512,512]{2,1,0:T(8,128)(2,1)} %all-gather.3.cloned.1.call-done, bf16[2,8,64,8,128]{4,3,1,2,0:T(8,128)(2,1)S(1)} %bitcast.95, bf16[128,128]{1,0:T(8,128)(2,1)S(1)} %copy-done.7), kind=kOutput, calls=%fused_computation.22 | convolution fusion | flops 1343225856 | bytes 10518528 | tf_op jit(solution)/shard_map/tpqd,cd->tpqc/dot_general | solution.py:39
  356.1 8.3 %add_convert_fusion = bf16[2,8,512,128]{3,2,1,0:T(8,128)(2,1)} fusion(f32[2,8,512,128]{3,2,1,0:T(8,128)} %fusion.14, bf16[2,8,512,128]{3,2,1,0:T(8,128)(2,1)} %param.11, f32[2,8,512,128]{3,2,1,0:T(8,128)} %get-tuple-element.6, bf16[128,128]{1,0:T(8,128)(2,1)S(1)} %copy-done.9, bf16[2,64,8,8,128]{4,3,2,1,0:T(8,128)(2,1)} %bitcast.101), kind=kOutput, calls=%fused_computation.19 | convolution fusion | flops 283115520 | bytes 14712832 | tf_op jit(solution)/shard_map/tpqd,cd->tpqc/dot_general | solution.py:41
  364.4 21.3 %reduce-scatter.5.cloned.1.call-done = bf16[8,128,512]{2,1,0:T(8,128)(2,1)} async-done(((bf16[8,512,512]{2,1,0:T(8,128)(2,1)}), bf16[8,128,512]{2,1,0:T(8,128)(2,1)}) %reduce-scatter.5.cloned.1.call-update) | async-done | bytes 1048592 | tf_op jit(solution)/shard_map/reduce_scatter | solution.py:47
  385.6 2.4 multiply_convert_fusion
  388.0 49.5 %reduce-scatter.3.cloned.1.call-done = bf16[8,128,512]{2,1,0:T(8,128)(2,1)} async-done(((bf16[8,512,512]{2,1,0:T(8,128)(2,1)}), bf16[8,128,512]{2,1,0:T(8,128)(2,1)}) %reduce-scatter.3.cloned.1.call-update) | async-done | bytes 1048592 | tf_op jit(solution)/shard_map/reduce_scatter | solution.py:51
  437.6 2.4 multiply_convert_fusion.1
  (8 shorter events, 0.0 us)
Async XLA Ops:
  7.2 1.6 copy-start
  7.2 1.6 copy-start.7
  7.2 56.1 %all-gather.3.cloned.1.call-start = ((), (), s32[]{:S(2)}) async-start(), calls=%async_computation.6 | async-start | bytes 5242880 | tf_op jit(solution)/shard_map/all_gather | solution.py:9
  7.9 157.9 %all-gather.5.cloned.1.call-start = ((), (), s32[]{:S(2)}) async-start(), calls=%async_computation.7 | async-start | bytes 5242880 | tf_op jit(solution)/shard_map/all_gather | solution.py:10
  8.7 377.0 %reduce-scatter.5.cloned.1.call-start = ((), (), s32[]{:S(2)}) async-start(), calls=%async_computation.9 | async-start | bytes 5242880 | tf_op jit(solution)/shard_map/reduce_scatter | solution.py:47
  228.5 2.3 copy-start.8
  228.5 2.3 copy-start.9
  228.8 5.8 %copy-start.6 = (bf16[2,512,8,128]{3,2,1,0:T(8,128)(2,1)}, bf16[2,512,8,128]{3,2,1,0:T(8,128)(2,1)S(1)}, u32[]{:S(2)}) copy-start(bf16[2,512,8,128]{3,2,1,0:T(8,128)(2,1)S(1)} %copy.55) | copy-start | bytes 6291460
  274.5 2.2 copy-start.2
  275.3 1.3 copy-start.4
  280.0 1.6 copy-start.5
  280.0 157.6 %reduce-scatter.3.cloned.1.call-start = ((), (), s32[]{:S(2)}) async-start(), calls=%async_computation.8 | async-start | bytes 5242880 | tf_op jit(solution)/shard_map/reduce_scatter | solution.py:51
  345.2 1.6 copy-start.3
  356.1 83.9 %copy-start.1 = (bf16[2,8,512,128]{3,2,1,0:T(8,128)(2,1)S(1)}, bf16[2,8,512,128]{3,2,1,0:T(8,128)(2,1)}, u32[]{:S(2)}) copy-start(bf16[2,8,512,128]{3,2,1,0:T(8,128)(2,1)} %param.6) | copy-start | bytes 6291460
Sparse Core Ops, SparseCore 0:
  9.8 53.3 all-gather.2
  65.1 94.5 all-gather.4
  280.1 105.4 reduce-scatter.4
  388.2 49.3 reduce-scatter.2
where the time goes:
time: 448 us; the launch traced here: 447 us
  blocking collectives  232 us (52%)
  waiting for transfers between devices  125 us (28%)
  matrix products  42.5 us (9%)
  local copies, waits for them, and re-layouts  28.8 us (6%)
  between operations  13.8 us (3%)
  other arithmetic  4.8 us (1%)
    all_to_all x1, blocking collectives, on_device(): lax.all_to_all(rowmix, 'seq', split_axis=2, concat_axis=1, tiled=True)  88.4 us
    all_to_all x1, blocking collectives, on_device(): lax.all_to_all(d_row_cols, 'seq', split_axis=1, concat_axis=2, tiled=True)  53.9 us
    all_gather x1, waiting for transfers between devices, on_device(): lax.all_gather(first_blocks, 'dp', axis=1, tiled=True)  52.5 us
    all_to_all x1, blocking collectives, on_device(): lax.all_to_all(colmix_cols, 'seq', split_axis=1, concat_axis=2, tiled=True)  50.9 us
    reduce_scatter x1, waiting for transfers between devices, on_device(): lax.psum_scatter(first_part.astype(jnp.bfloat16), 'dp', scatter_dimension...  49.5 us
    all_to_all x1, blocking collectives, on_device(): lax.all_to_all(d_col, 'seq', split_axis=2, concat_axis=1, tiled=True)  38.6 us
    reduce_scatter x1, waiting for transfers between devices, on_device(): lax.psum_scatter(second_part.astype(jnp.bfloat16), 'dp', scatter_dimensio...  21.3 us
  transfers between devices with their start and end apart: 4, of which 3 were waited for; matrix products, arithmetic and copies ran while one was open for 10% of the time, Pallas kernels for 0%

commit v1 on v0

--- a/solution.py
+++ b/solution.py
@@ -6,7 +6,9 @@
 
 def on_device(traces_in, w_value, w_gate, first_blocks, second_blocks, cotangent):
     full_first, full_second = (
-        lax.all_gather(first_blocks, "dp", axis=1, tiled=True),
+        jnp.concatenate(
+            lax.all_to_all(jnp.stack([first_blocks] * lax.axis_size("dp")), "dp", 0, 0), axis=1
+        ),
         lax.all_gather(second_blocks, "dp", axis=1, tiled=True),
     )
     values = jnp.einsum(

time: 448 us -> 441 us (0.984)
  blocking collectives: 232 us -> 191 us
  waiting for transfers between devices: 125 us -> 145 us
  local copies, waits for them, and re-layouts: 28.8 us -> 37.2 us
  starting transfers between devices: 0.16 us -> 8.26 us
    all_to_all x0 -> x1, waiting for transfers between devices: none -> 72 us  [on_device(): lax.all_to_all(jnp.stack([first_blocks] * lax.axis_size('dp')), 'dp', 0, 0)]
    all_gather x1 -> x0, waiting for transfers between devices: 52.5 us -> none  [on_device(): lax.all_gather(first_blocks, 'dp', axis=1, tiled=True)]
    all_to_all x1, blocking collectives: 88.4 us -> 65.4 us  [on_device(): lax.all_to_all(rowmix, 'seq', split_axis=2, concat_axis=1, tiled=True)]
    all_to_all x1, blocking collectives: 53.9 us -> 40.2 us  [on_device(): lax.all_to_all(d_row_cols, 'seq', split_axis=1, concat_axis=2, tiled=True)]
    all_to_all x0 -> x1, starting transfers between devices: none -> 8.18 us  [on_device(): lax.all_to_all(jnp.stack([first_blocks] * lax.axis_size('dp')), 'dp', 0, 0)]
where the time goes in v1:
time: 441 us; the launch traced here: 440 us
  blocking collectives  191 us (43%)
  waiting for transfers between devices  145 us (33%)
  matrix products  39.8 us (9%)
  local copies, waits for them, and re-layouts  37.2 us (8%)
  between operations  13.8 us (3%)
  starting transfers between devices  8.26 us (2%)
  other arithmetic  4.8 us (1%)
    all_to_all x1, waiting for transfers between devices, on_device(): lax.all_to_all(jnp.stack([first_blocks] * lax.axis_size('dp')), 'dp', 0, 0)  72 us
    all_to_all x1, blocking collectives, on_device(): lax.all_to_all(rowmix, 'seq', split_axis=2, concat_axis=1, tiled=True)  65.4 us
    reduce_scatter x1, waiting for transfers between devices, on_device(): lax.psum_scatter(first_part.astype(jnp.bfloat16), 'dp', scatter_dimension...  50.3 us
    all_to_all x1, blocking collectives, on_device(): lax.all_to_all(colmix_cols, 'seq', split_axis=1, concat_axis=2, tiled=True)  47.5 us
    all_to_all x1, blocking collectives, on_device(): lax.all_to_all(d_row_cols, 'seq', split_axis=1, concat_axis=2, tiled=True)  40.2 us
    all_to_all x1, blocking collectives, on_device(): lax.all_to_all(d_col, 'seq', split_axis=2, concat_axis=1, tiled=True)  38.1 us
    reduce_scatter x1, waiting for transfers between devices, on_device(): lax.psum_scatter(second_part.astype(jnp.bfloat16), 'dp', scatter_dimensio...  21.9 us
  transfers between devices with their start and end apart: 4, of which 3 were waited for; matrix products, arithmetic and copies ran while one was open for 10% of the time, Pallas kernels for 0%

profile of v1, /device:TPU:1, one launch (start us, length us, event | category | flops | bytes accessed | tf_op | source)
XLA Modules:
  0.0 440.1 jit_solution(4972691665759616952)
XLA Ops:
  7.2 0.0 copy-start
  7.2 3.9 stack.2
  11.0 8.2 %all-to-all-start = ((bf16[4,8,128,512]{3,2,1,0:T(8,128)(2,1)}), bf16[4,8,128,512]{3,2,1,0:T(8,128)(2,1)}, u32[]{:S(2)}, u32[]{:S(2)}) async-start(bf16[4,8,128,512]{3,2,1,0:T(8,128)(2,1)} %stack.2), calls=%async_computation | async-start | bytes 8388608 | tf_op jit(solution)/shard_map/all_to_all | solution.py:10
  19.2 0.0 all-gather.2.cloned.1.call-start
  19.2 0.7 all-gather.2.cloned.1.call-update
  19.9 0.0 reduce-scatter.5.cloned.1.call-start
  20.0 0.0 copy-done
  20.0 0.0 copy-done.9
  20.0 2.0 convolution_convert_fusion
  22.0 72.0 %all-to-all-done = bf16[4,8,128,512]{3,2,1,0:T(8,128)(2,1)} async-done(((bf16[4,8,128,512]{3,2,1,0:T(8,128)(2,1)}), bf16[4,8,128,512]{3,2,1,0:T(8,128)(2,1)}, u32[]{:S(2)}, u32[]{:S(2)}) %all-to-all-start) | async-done | bytes 4194336 | tf_op jit(solution)/shard_map/all_to_all | solution.py:10
  94.0 2.6 copy.50
  96.6 0.0 copy-start.2
  96.6 1.9 copy-done.2
  98.5 0.0 copy-done.4
  98.5 2.8 convert_bitcast_fusion.3
  101.3 6.2 %copy.52 = bf16[2,8,512,128]{3,0,1,2:T(2,128)(2,1)} copy(bf16[2,8,512,128]{2,3,0,1:T(8,128)(2,1)} %convert_bitcast_fusion.3) | data formatting | bytes 4194304 | tf_op jit(solution)/shard_map/convert_element_type | solution.py:22
  107.5 65.4 %all_to_all.68 = bf16[2,8,512,128]{3,0,1,2:T(2,128)(2,1)S(1)} all-to-all(bf16[2,8,512,128]{3,0,1,2:T(2,128)(2,1)} %copy.52), channel_id=1, replica_groups=mesh['dp'=4,'seq'=64] {'seq'}, dimensions={2} | all-to-all | bytes 4194304 | tf_op jit(solution)/shard_map/all_to_all | solution.py:25
  172.9 0.5 copy.105
  173.5 1.9 copy.54
  175.4 5.6 %convert_bitcast_fusion.2 = bf16[2,512,8,128]{1,3,0,2:T(8,128)(2,1)} fusion(bf16[8,512,512]{2,1,0:T(8,128)(2,1)} %all-gather.2.cloned.1.call-done, bf16[2,512,8,128]{3,2,1,0:T(8,128)(2,1)} %bitcast.89), kind=kOutput, calls=%fused_computation.30 | convolution fusion | flops 1074790400 | bytes 8388608 | tf_op jit(solution)/shard_map/qij,tjqc->tiqc/dot_general | solution.py:26
  181.0 6.2 %copy.56 = bf16[2,512,8,128]{3,0,2,1:T(2,128)(2,1)} copy(bf16[2,512,8,128]{1,3,0,2:T(8,128)(2,1)} %convert_bitcast_fusion.2) | data formatting | bytes 4194304 | tf_op jit(solution)/shard_map/convert_element_type | solution.py:29
  187.2 47.5 %all_to_all.69 = bf16[2,512,8,128]{3,0,2,1:T(2,128)(2,1)S(1)} all-to-all(bf16[2,512,8,128]{3,0,2,1:T(2,128)(2,1)} %copy.56), channel_id=1, replica_groups=mesh['dp'=4,'seq'=64] {'seq'}, dimensions={1} | all-to-all | bytes 4194304 | tf_op jit(solution)/shard_map/all_to_all | solution.py:30
  234.7 0.3 copy.57
  235.0 0.0 copy-start.8
  235.0 2.1 copy-done.10
  237.1 3.7 fusion
  240.8 0.0 copy-done.8
  240.8 1.4 copy.59
  242.1 38.1 %all_to_all.70 = bf16[2,8,512,128]{3,1,0,2:T(8,128)(2,1)S(1)} all-to-all(bf16[2,8,512,128]{3,1,0,2:T(8,128)(2,1)S(1)} %copy.59), channel_id=1, replica_groups=mesh['dp'=4,'seq'=64] {'seq'}, dimensions={2} | all-to-all | bytes 4194304 | tf_op jit(solution)/shard_map/all_to_all | solution.py:31
  280.2 0.8 copy.61
  281.1 1.3 copy-done.6
  282.4 3.3 bitcast_convert_fusion
  285.7 0.0 reduce-scatter.5.cloned.1.call-update
  285.7 0.0 reduce-scatter.3.cloned.1.call-start
  285.8 1.5 copy-done.7
  287.3 4.8 %convert_bitcast_fusion.1 = bf16[2,512,8,128]{1,3,0,2:T(8,128)(2,1)} fusion(bf16[8,512,512]{2,1,0:T(8,128)(2,1)} %all-gather.2.cloned.1.call-done, bf16[2,512,8,128]{3,2,1,0:T(8,128)(2,1)S(1)} %bitcast.94), kind=kOutput, calls=%fused_computation.29 | convolution fusion | flops 1074790400 | bytes 8388608 | tf_op jit(solution)/shard_map/qij,tiqc->tjqc/dot_general | solution.py:32
  292.1 4.9 %copy.63 = bf16[2,512,8,128]{3,0,2,1:T(2,128)(2,1)S(1)} copy(bf16[2,512,8,128]{1,3,0,2:T(8,128)(2,1)} %convert_bitcast_fusion.1) | data formatting | bytes 4194304 | tf_op jit(solution)/shard_map/convert_element_type | solution.py:33
  297.1 40.2 %all_to_all.71 = bf16[2,512,8,128]{3,0,2,1:T(2,128)(2,1)S(1)} all-to-all(bf16[2,512,8,128]{3,0,2,1:T(2,128)(2,1)S(1)} %copy.63), channel_id=1, replica_groups=mesh['dp'=4,'seq'=64] {'seq'}, dimensions={1} | all-to-all | bytes 4194304 | tf_op jit(solution)/shard_map/all_to_all | solution.py:34
  337.3 0.3 copy.64
  337.6 1.3 copy-done.5
  338.9 3.3 bitcast_convert_fusion.1
  342.2 0.0 reduce-scatter.3.cloned.1.call-update
  342.2 6.0 %fusion.10 = f32[2,8,512,128]{3,2,1,0:T(8,128)} fusion(bf16[8,512,512,1]{2,1,0,3:T(8,128)(2,1)} %bitcast.88, bf16[2,8,64,8,128]{4,3,1,2,0:T(8,128)(2,1)S(1)} %bitcast.92, bf16[128,128]{1,0:T(8,128)(2,1)S(1)} %copy-done.9), kind=kOutput, calls=%fused_computation.18 | convolution fusion | flops 1343225856 | bytes 10518528 | tf_op jit(solution)/shard_map/tpqd,cd->tpqc/dot_general | solution.py:41
  348.2 8.3 %add_convert_fusion = bf16[2,8,512,128]{3,2,1,0:T(8,128)(2,1)} fusion(f32[2,8,512,128]{3,2,1,0:T(8,128)} %fusion.10, bf16[2,8,512,128]{3,2,1,0:T(8,128)(2,1)} %param.11, f32[2,8,512,128]{3,2,1,0:T(8,128)} %get-tuple-element.6, bf16[128,128]{1,0:T(8,128)(2,1)S(1)} %copy-done.11, bf16[2,64,8,8,128]{4,3,2,1,0:T(8,128)(2,1)} %bitcast.98), kind=kOutput, calls=%fused_computation.15 | convolution fusion | flops 283115520 | bytes 14712832 | tf_op jit(solution)/shard_map/tpqd,cd->tpqc/dot_general | solution.py:43
  356.5 21.9 %reduce-scatter.5.cloned.1.call-done = bf16[8,128,512]{2,1,0:T(8,128)(2,1)} async-done(((bf16[8,512,512]{2,1,0:T(8,128)(2,1)}), bf16[8,128,512]{2,1,0:T(8,128)(2,1)}) %reduce-scatter.5.cloned.1.call-update) | async-done | bytes 1048592 | tf_op jit(solution)/shard_map/reduce_scatter | solution.py:49
  378.4 2.4 multiply_convert_fusion
  380.8 50.3 %reduce-scatter.3.cloned.1.call-done = bf16[8,128,512]{2,1,0:T(8,128)(2,1)} async-done(((bf16[8,512,512]{2,1,0:T(8,128)(2,1)}), bf16[8,128,512]{2,1,0:T(8,128)(2,1)}) %reduce-scatter.3.cloned.1.call-update) | async-done | bytes 1048592 | tf_op jit(solution)/shard_map/reduce_scatter | solution.py:53
  431.2 2.4 multiply_convert_fusion.1
  (13 shorter events, 0.0 us)
Async XLA Ops:
  7.2 12.8 %copy-start = (bf16[2,8,512,128]{3,2,1,0:T(8,128)(2,1)S(1)}, bf16[2,8,512,128]{3,2,1,0:T(8,128)(2,1)}, u32[]{:S(2)}) copy-start(bf16[2,8,512,128]{3,2,1,0:T(8,128)(2,1)} %param.6) | copy-start | bytes 6291460
  11.0 9.0 %copy-start.9 = (bf16[128,128]{1,0:T(8,128)(2,1)S(1)}, bf16[128,128]{1,0:T(8,128)(2,1)}, u32[]{:S(2)}) copy-start(bf16[128,128]{1,0:T(8,128)(2,1)} %param.7) | copy-start | bytes 98308
  11.0 82.9 %all-to-all-start = ((bf16[4,8,128,512]{3,2,1,0:T(8,128)(2,1)}), bf16[4,8,128,512]{3,2,1,0:T(8,128)(2,1)}, u32[]{:S(2)}, u32[]{:S(2)}) async-start(bf16[4,8,128,512]{3,2,1,0:T(8,128)(2,1)} %stack.2), calls=%async_computation | async-start | bytes 8388608 | tf_op jit(solution)/shard_map/all_to_all | solution.py:10
  19.2 156.2 %all-gather.2.cloned.1.call-start = ((), (), s32[]{:S(2)}) async-start(), calls=%async_computation.7 | async-start | bytes 5242880 | tf_op jit(solution)/shard_map/all_gather | solution.py:12
  19.9 358.5 %reduce-scatter.5.cloned.1.call-start = ((), (), s32[]{:S(2)}) async-start(), calls=%async_computation.9 | async-start | bytes 5242880 | tf_op jit(solution)/shard_map/reduce_scatter | solution.py:49
  94.0 4.6 %copy-start.4 = (bf16[2,8,512,128]{3,2,1,0:T(8,128)(2,1)S(1)}, bf16[2,8,512,128]{3,2,1,0:T(8,128)(2,1)}, u32[]{:S(2)}) copy-start(bf16[2,8,512,128]{3,2,1,0:T(8,128)(2,1)} %convolution_convert_fusion) | copy-start | bytes 6291460
  96.6 2.0 copy-start.2
  234.7 2.3 copy-start.10
  234.7 2.3 copy-start.11
  235.0 5.8 %copy-start.8 = (bf16[2,512,8,128]{3,2,1,0:T(8,128)(2,1)}, bf16[2,512,8,128]{3,2,1,0:T(8,128)(2,1)S(1)}, u32[]{:S(2)}) copy-start(bf16[2,512,8,128]{3,2,1,0:T(8,128)(2,1)S(1)} %copy.57) | copy-start | bytes 6291460
  280.2 2.2 copy-start.3
  281.1 1.3 copy-start.6
  285.7 1.6 copy-start.7
  285.7 145.4 %reduce-scatter.3.cloned.1.call-start = ((), (), s32[]{:S(2)}) async-start(), calls=%async_computation.8 | async-start | bytes 5242880 | tf_op jit(solution)/shard_map/reduce_scatter | solution.py:53
  337.3 1.6 copy-start.5
  348.2 85.3 %copy-start.1 = (bf16[2,8,512,128]{3,2,1,0:T(8,128)(2,1)S(1)}, bf16[2,8,512,128]{3,2,1,0:T(8,128)(2,1)}, u32[]{:S(2)}) copy-start(bf16[2,8,512,128]{3,2,1,0:T(8,128)(2,1)} %param.6) | copy-start | bytes 6291460
Sparse Core Ops, SparseCore 0:
  21.8 78.8 all-gather.1
  285.8 92.5 reduce-scatter.4
  381.1 49.9 reduce-scatter.2
